TPU v7x, 256 devices: a whole 4x4x8 slice. The times are simulated.
256 devices in a mesh: row: 16 (over x_lo, y, core), col: 16 (over z, x_hi).
Axes of the slice: x: 4 (x_hi: 2, x_lo: 2; x = x_hi * 2 + x_lo), y: 4, z: 8, core: 2. Of those that a mesh axis runs over, the one named last changes fastest.
Arguments:
- green: bfloat16 [32768, 32768], P('row', 'col'), may hold values from -0.046875 to 0.046875
- mask: int32 [128, 128], P('row', 'col'), may hold values from 0 to 1, as said below
- probes: bfloat16 [32768, 256], P('col', 'row'), may hold values from -6 to 6
Outputs:
- sketch: float32 [32768, 256], P('row', 'col')
- adjoint: float32 [32768, 256], P('col', 'row')
Inputs may be any that keep to these rules, and one draw needn't show every extreme that they name: `mask`: block row i belongs to gauge i % 6 and time block i // 6; block column j to window j // 8. A block is 1 when its time block is no earlier than the window's onset plus a travel delay of its gauge and subfault block.
All inputs are finite; a program needn't handle non-finite values.
Results may differ from a plain program's by a relative error of at most 0.0022.
Values may be sent and summed in bfloat16 or wider, within the bound.
A program may use at most 128 MiB of HBM per device.

v0:
```python
import jax
import jax.numpy as jnp
from jax import lax
from jax.sharding import PartitionSpec as P


def local(green, mask, probes):
    row_blocks, col_blocks = mask.shape
    block_size = green.shape[0] // row_blocks
    shaped = green.reshape(row_blocks, block_size, col_blocks, block_size)
    tiles = (shaped * mask.astype(jnp.bfloat16)[:, None, :, None]).reshape(green.shape)
    all_probes = lax.all_gather(probes, "row", axis=1, tiled=True)
    partial_sketch = jnp.dot(tiles, all_probes, preferred_element_type=jnp.float32)
    own_sketch = lax.psum_scatter(partial_sketch, "col", scatter_dimension=1, tiled=True)
    lowered = lax.all_gather(own_sketch.astype(jnp.bfloat16), "col", axis=1, tiled=True)
    term_t = lax.dot_general(
        lowered, tiles, (((0,), (0,)), ((), ())), preferred_element_type=jnp.float32
    )
    adjoint_t = lax.psum_scatter(term_t, "row", scatter_dimension=0, tiled=True)
    return (own_sketch, adjoint_t.T)


def solution(mesh):
    in_specs = (P("row", "col"), P("row", "col"), P("col", "row"))
    out_specs = (P("row", "col"), P("col", "row"))
    return jax.shard_map(local, mesh=mesh, in_specs=in_specs, out_specs=out_specs, check_vma=False)
```

profile of v0, /device:TPU:32, one launch (start us, length us, event | category | flops | bytes accessed | tf_op | source)
XLA Modules:
  0.0 419.4 jit_solution(13793577123540415991)
XLA Ops:
  7.2 0.0 all-gather.3.cloned.1.call-start
  7.2 0.7 all-gather.3.cloned.1.call-update
  7.9 0.0 reduce-scatter.3.cloned.1.call-start
  7.9 0.7 convert_element_type.6
  8.6 3.8 mul.11
  12.5 10.3 %copy.5 = bf16[256,8,8,256]{3,1,2,0:T(8,128)(2,1)} copy(bf16[256,8,8,256]{3,2,1,0:T(8,128)(2,1)} %bitcast.9) | data formatting | bytes 16777216
  22.8 10.5 %mul.13 = bf16[2048,2048]{1,0:T(8,128)(2,1)} multiply(bf16[2048,2048]{1,0:T(8,128)(2,1)} %param.3, bf16[2048,2048]{1,0:T(8,128)(2,1)} %bitcast.8) | non-fusion elementwise | flops 4194304 | bytes 25165824 | tf_op jit(solution)/shard_map/mul | solution.py:11
  33.3 14.2 %all-gather.3.cloned.1.call-done = bf16[2048,256]{0,1:T(8,128)(2,1)} async-done(((bf16[2048,16]{0,1:T(8,128)(2,1)}), bf16[2048,256]{0,1:T(8,128)(2,1)}) %all-gather.3.cloned.1.call-update) | async-done | bytes 1048592 | tf_op jit(solution)/shard_map/all_gather | solution.py:12
  47.5 7.3 %fusion = f32[2048,256]{0,1:T(8,128)} fusion(bf16[2048,2048]{1,0:T(8,128)(2,1)} %mul.13, bf16[2048,256]{0,1:T(8,128)(2,1)} %all-gather.3.cloned.1.call-done), kind=kOutput, calls=%fused_computation | convolution fusion | flops 2147483648 | bytes 11534336 | tf_op jit(solution)/shard_map/dot_general | solution.py:13
  54.8 0.0 reduce-scatter.3.cloned.1.call-update
  54.8 0.0 all-gather.5.cloned.1.call-start
  54.9 207.1 %reduce-scatter.3.cloned.1.call-done = f32[2048,16]{0,1:T(8,128)} async-done(((f32[2048,256]{0,1:T(8,128)}), f32[2048,16]{0,1:T(8,128)}) %reduce-scatter.3.cloned.1.call-update) | async-done | bytes 131088 | tf_op jit(solution)/shard_map/reduce_scatter | solution.py:14
  262.0 1.5 convert_element_type.7
  263.5 0.0 all-gather.5.cloned.1.call-update
  263.5 0.0 reduce-scatter.5.cloned.1.call-start
  263.6 78.4 %all-gather.5.cloned.1.call-done = bf16[2048,256]{0,1:T(8,128)(2,1)} async-done(((bf16[2048,16]{0,1:T(8,128)(2,1)}), bf16[2048,256]{0,1:T(8,128)(2,1)}) %all-gather.5.cloned.1.call-update) | async-done | bytes 1048592 | tf_op jit(solution)/shard_map/all_gather | solution.py:15
  341.9 7.4 %fusion.1 = f32[256,2048]{1,0:T(8,128)} fusion(bf16[2048,256]{0,1:T(8,128)(2,1)} %all-gather.5.cloned.1.call-done, bf16[2048,2048]{1,0:T(8,128)(2,1)} %mul.13), kind=kOutput, calls=%fused_computation.1 | convolution fusion | flops 2147483648 | bytes 11534336 | tf_op jit(solution)/shard_map/dot_general | solution.py:16
  349.3 0.0 reduce-scatter.5.cloned.1.call-update
  349.4 63.5 %reduce-scatter.5.cloned.1.call-done = f32[16,2048]{1,0:T(8,128)} async-done(((f32[256,2048]{1,0:T(8,128)}), f32[16,2048]{1,0:T(8,128)}) %reduce-scatter.5.cloned.1.call-update) | async-done | bytes 131088 | tf_op jit(solution)/shard_map/reduce_scatter | solution.py:19
Async XLA Ops:
  7.2 40.3 %all-gather.3.cloned.1.call-start = ((), (), s32[]{:S(2)}) async-start(), calls=%async_computation.2 | async-start | bytes 1114112 | tf_op jit(solution)/shard_map/all_gather | solution.py:12
  7.9 254.1 %reduce-scatter.3.cloned.1.call-start = ((), (), s32[]{:S(2)}) async-start(), calls=%async_computation.3 | async-start | bytes 2228224 | tf_op jit(solution)/shard_map/reduce_scatter | solution.py:14
  54.8 287.1 %all-gather.5.cloned.1.call-start = ((), (), s32[]{:S(2)}) async-start(), calls=%async_computation.4 | async-start | bytes 1114112 | tf_op jit(solution)/shard_map/all_gather | solution.py:15
  263.5 149.3 %reduce-scatter.5.cloned.1.call-start = ((), (), s32[]{:S(2)}) async-start(), calls=%async_computation.5 | async-start | bytes 2228224 | tf_op jit(solution)/shard_map/reduce_scatter | solution.py:19
Sparse Core Ops, SparseCore 0:
  9.8 37.5 all-gather.2
  55.0 206.9 reduce-scatter.2
  265.1 76.7 all-gather.4
  349.5 63.3 reduce-scatter.4
where the time goes:
time: 420 us; the launch traced here: 419 us
  waiting for transfers between devices  364 us (87%)
  matrix products  14.7 us (4%)
  local copies, waits for them, and re-layouts  14.1 us (3%)
  between operations  13.8 us (3%)
  other arithmetic  12.8 us (3%)
    reduce_scatter x1, waiting for transfers between devices, local(): lax.psum_scatter(partial_sketch, 'col', scatter_dimension=1, tiled=True)  207 us
    all_gather x1, waiting for transfers between devices, local(): lax.all_gather(own_sketch.astype(jnp.bfloat16), 'col', axis=1, tiled=True)  78.4 us
    reduce_scatter x1, waiting for transfers between devices, local(): adjoint_t = lax.psum_scatter(term_t, 'row', scatter_dimension=0, tiled=True)  63.5 us
    all_gather x1, waiting for transfers between devices, local(): all_probes = lax.all_gather(probes, 'row', axis=1, tiled=True)  14.2 us
    mul x1, other arithmetic, local(): shaped * mask.astype(jnp.bfloat16)[:, None, :, None]  10.5 us
    unnamed x1, local copies, waits for them, and re-layouts  10.3 us
  transfers between devices with their start and end apart: 4, of which 4 were waited for; matrix products, arithmetic and copies ran while one was open for 6% of the time, Pallas kernels for 0%

commit v1 on v0

--- a/solution.py
+++ b/solution.py
@@ -12,7 +12,12 @@
     all_probes = lax.all_gather(probes, "row", axis=1, tiled=True)
     partial_sketch = jnp.dot(tiles, all_probes, preferred_element_type=jnp.float32)
     own_sketch = lax.psum_scatter(partial_sketch, "col", scatter_dimension=1, tiled=True)
-    lowered = lax.all_gather(own_sketch.astype(jnp.bfloat16), "col", axis=1, tiled=True)
+    lowered = jnp.concatenate(
+        lax.all_to_all(
+            jnp.stack([own_sketch.astype(jnp.bfloat16)] * lax.axis_size("col")), "col", 0, 0
+        ),
+        axis=1,
+    )
     term_t = lax.dot_general(
         lowered, tiles, (((0,), (0,)), ((), ())), preferred_element_type=jnp.float32
     )

time: 420 us -> 369 us (0.88)
  waiting for transfers between devices: 364 us -> 284 us
  blocking collectives: 0 us -> 30.3 us
    all_gather x1 -> x0, waiting for transfers between devices: 78.4 us -> none  [local(): lax.all_gather(own_sketch.astype(jnp.bfloat16), 'col', axis=1, tiled=True)]
    all_to_all x0 -> x1, blocking collectives: none -> 30.3 us  [local(): lax.all_to_all(jnp.stack([own_sketch.astype(jnp.bfloat16)] * lax.axis_siz...]
  transfers between devices with their start and end apart: 4 -> 3, of which waited for: 4 -> 3; matrix products, arithmetic and copies ran while one was open for 6% -> 7% of each run, Pallas kernels for 0% -> 0%
where the time goes in v1:
time: 369 us
  waiting for transfers between devices  284 us (77%)
  blocking collectives  30.3 us (8%)
  matrix products  14.4 us (4%)
  local copies, waits for them, and re-layouts  14.2 us (4%)
  between operations  13.8 us (4%)
  other arithmetic  12.1 us (3%)
    reduce_scatter x1, waiting for transfers between devices, local(): lax.psum_scatter(partial_sketch, 'col', scatter_dimension=1, tiled=True)  207 us
    reduce_scatter x1, waiting for transfers between devices, local(): adjoint_t = lax.psum_scatter(term_t, 'row', scatter_dimension=0, tiled=True)  62.4 us
    all_to_all x1, blocking collectives, local(): lax.all_to_all(jnp.stack([own_sketch.astype(jnp.bfloat16)] * lax.axis_siz...  30.3 us
    all_gather x1, waiting for transfers between devices, local(): all_probes = lax.all_gather(probes, 'row', axis=1, tiled=True)  14.2 us
    mul x1, other arithmetic, local(): shaped * mask.astype(jnp.bfloat16)[:, None, :, None]  10.5 us
    unnamed x1, local copies, waits for them, and re-layouts  10.3 us
  transfers between devices with their start and end apart: 3, of which 3 were waited for; matrix products, arithmetic and copies ran while one was open for 7% of the time, Pallas kernels for 0%

profile of v1, /device:TPU:32, one launch (start us, length us, event | category | flops | bytes accessed | tf_op | source)
XLA Modules:
  0.0 369.2 jit_solution(15955650981381141620)
XLA Ops:
  7.2 0.0 all-gather.2.cloned.1.call-start
  7.2 0.7 all-gather.2.cloned.1.call-update
  7.9 0.0 reduce-scatter.3.cloned.1.call-start
  7.9 0.7 convert_element_type.6
  8.6 3.8 %mul.11 = bf16[8,256,8,256]{3,2,1,0:T(8,128)(2,1)} broadcast(bf16[8,8]{1,0:T(8,128)(2,1)S(1)} %convert_element_type.6), dimensions={0,2} | broadcast | bytes 8388736 | tf_op jit(solution)/shard_map/mul | solution.py:11
  12.5 10.3 %copy.6 = bf16[256,8,8,256]{3,1,2,0:T(8,128)(2,1)} copy(bf16[256,8,8,256]{3,2,1,0:T(8,128)(2,1)} %bitcast.12) | data formatting | bytes 16777216
  22.7 10.5 %mul.13 = bf16[2048,2048]{1,0:T(8,128)(2,1)} multiply(bf16[2048,2048]{1,0:T(8,128)(2,1)} %param.3, bf16[2048,2048]{1,0:T(8,128)(2,1)} %bitcast.11) | non-fusion elementwise | flops 4194304 | bytes 25165824 | tf_op jit(solution)/shard_map/mul | solution.py:11
  33.3 14.2 %all-gather.2.cloned.1.call-done = bf16[2048,256]{0,1:T(8,128)(2,1)} async-done(((bf16[2048,16]{0,1:T(8,128)(2,1)}), bf16[2048,256]{0,1:T(8,128)(2,1)}) %all-gather.2.cloned.1.call-update) | async-done | bytes 1048592 | tf_op jit(solution)/shard_map/all_gather | solution.py:12
  47.5 7.3 %fusion = f32[2048,256]{0,1:T(8,128)} fusion(bf16[2048,2048]{1,0:T(8,128)(2,1)} %mul.13, bf16[2048,256]{0,1:T(8,128)(2,1)} %all-gather.2.cloned.1.call-done), kind=kOutput, calls=%fused_computation | convolution fusion | flops 2147483648 | bytes 11534336 | tf_op jit(solution)/shard_map/dot_general | solution.py:13
  54.8 0.0 reduce-scatter.3.cloned.1.call-update
  54.8 0.0 reduce-scatter.5.cloned.1.call-start
  54.9 206.9 %reduce-scatter.3.cloned.1.call-done = f32[2048,16]{0,1:T(8,128)} async-done(((f32[2048,256]{0,1:T(8,128)}), f32[2048,16]{0,1:T(8,128)}) %reduce-scatter.3.cloned.1.call-update) | async-done | bytes 131088 | tf_op jit(solution)/shard_map/reduce_scatter | solution.py:14
  261.8 0.9 convert_element_type.7
  262.7 0.1 stack.2
  262.9 30.3 %all_to_all.5 = bf16[16,2048,16]{1,2,0:T(8,128)(2,1)S(1)} all-to-all(bf16[16,2048,16]{1,2,0:T(8,128)(2,1)S(1)} %stack.2), channel_id=1, replica_groups=mesh['row'=16,'col'=16] {'col'}, dimensions={0} | all-to-all | bytes 2097152 | tf_op jit(solution)/shard_map/all_to_all | solution.py:16
  293.2 7.1 %fusion.1 = f32[256,2048]{1,0:T(8,128)} fusion(bf16[2048,256]{0,1:T(8,128)(2,1)S(1)} %bitcast.13, bf16[2048,2048]{1,0:T(8,128)(2,1)} %mul.13), kind=kOutput, calls=%fused_computation.1 | convolution fusion | flops 2147483648 | bytes 11534336 | tf_op jit(solution)/shard_map/dot_general | solution.py:21
  300.2 0.0 reduce-scatter.5.cloned.1.call-update
  300.3 62.4 %reduce-scatter.5.cloned.1.call-done = f32[16,2048]{1,0:T(8,128)} async-done(((f32[256,2048]{1,0:T(8,128)}), f32[16,2048]{1,0:T(8,128)}) %reduce-scatter.5.cloned.1.call-update) | async-done | bytes 131088 | tf_op jit(solution)/shard_map/reduce_scatter | solution.py:24
Async XLA Ops:
  7.2 40.3 %all-gather.2.cloned.1.call-start = ((), (), s32[]{:S(2)}) async-start(), calls=%async_computation.3 | async-start | bytes 1114112 | tf_op jit(solution)/shard_map/all_gather | solution.py:12
  7.9 253.9 %reduce-scatter.3.cloned.1.call-start = ((), (), s32[]{:S(2)}) async-start(), calls=%async_computation.4 | async-start | bytes 2228224 | tf_op jit(solution)/shard_map/reduce_scatter | solution.py:14
  54.8 307.8 %reduce-scatter.5.cloned.1.call-start = ((), (), s32[]{:S(2)}) async-start(), calls=%async_computation.5 | async-start | bytes 2228224 | tf_op jit(solution)/shard_map/reduce_scatter | solution.py:24
Sparse Core Ops, SparseCore 0:
  9.8 37.5 all-gather.1
  55.0 206.8 reduce-scatter.2
  300.4 62.2 reduce-scatter.4
